TPU v7x, 128 devices: a whole 4x4x4 slice. The times are simulated.
128 devices in a mesh: dp: 4 (over x_lo, core), seq: 32 (over y, x_hi, z).
Axes of the slice: x: 4 (x_hi: 2, x_lo: 2; x = x_hi * 2 + x_lo), y: 4, z: 4, core: 2. Of those that a mesh axis runs over, the one named last changes fastest.
Arguments:
- embeddings: bfloat16 [4, 32, 512, 8192], P('dp', 'seq'), may hold values from -6 to 6
- layout: int32 [4, 32, 32], P('dp'), may hold values from 0 to 31, as said below
- lengths: int32 [4], P('dp'), may hold values from 4096 to 16384, as said below
- targets: int32 [4, 4096, 2048], P('dp', 'seq'), may hold values from 0 to 7
- projection: bfloat16 [8192, 768], P('dp'), may hold values from -0.0625 to 0.0625
- kernels: bfloat16 [2, 3, 768, 384], replicated, may hold values from -0.125 to 0.125
- mixers: bfloat16 [2, 384, 768], replicated, may hold values from -0.3125 to 0.3125
- readout: bfloat16 [768, 2048], replicated, may hold values from -0.21875 to 0.21875
Outputs:
- kernel_grads: float32 [2, 3, 768, 384], P(None, None, 'seq', 'dp')
- mixer_grads: float32 [2, 384, 768], P(None, 'seq', 'dp')
- readout_grad: float32 [768, 2048], P('seq', 'dp')
- trunk_grad: float32 [4, 8192, 768], P('dp', 'seq')
Inputs may be any that keep to these rules, and one draw needn't show every extreme that they name: For every window w and shard j, layout[w, s, j] over all shards s lists every block number once. `lengths`: multiples of 128; in every draw one window has the full 16384 and another the least.
All inputs are finite; a program needn't handle non-finite values.
Results may differ from a plain program's by a relative error of at most 0.017.
Values may be sent and summed in bfloat16 or wider, within the bound.
A program may use at most 128 MiB of HBM per device.

v0:
```python
import math

import jax
import jax.numpy as jnp
from jax import lax
from jax.experimental import pallas as pl
from jax.experimental.pallas import tpu as pltpu
from jax.sharding import PartitionSpec as P

MESH = pl.DeviceIdType.MESH
CHUNK = 512
STAGES = ((0, 512, 96), (1280, 256, 64))
STAGE_ROWS = (1280, 768)
GROUPS = (
    (((0, 1, 2), 128), ((1, 2, 0), 128), ((2, 0, 1), 128)),
    (((0, 1, 2), 128), ((1, 2, 0), 128), ((2, 0, 1), 128)),
    (((1, 0, 2), 256), ((0, 1, 2), 256)),
)


def place():
    dp, seq = lax.axis_index("dp"), lax.axis_index("seq")
    core = lax.rem(dp, 2)
    x = lax.rem(lax.div(seq, 4), 2) * 2 + lax.div(dp, 2)
    return (x, lax.div(seq, 8), lax.rem(seq, 4)), core


def device_at(coords, core):
    x, y, z = coords
    return (lax.rem(x, 2) * 2 + core, y * 8 + lax.div(x, 2) * 4 + z)


def moved(coords, axis, step):
    out = list(coords)
    out[axis] = lax.rem(out[axis] + step, 4)
    return tuple(out)


class Sender:
    def __init__(self, send_sems, recv_sems):
        self.send_sems, self.recv_sems, self.copies = send_sems, recv_sems, []

    def __call__(self, src, dst, device):
        at = len(self.copies)
        copy = pltpu.make_async_remote_copy(
            src_ref=src,
            dst_ref=dst,
            send_sem=self.send_sems.at[at],
            recv_sem=self.recv_sems.at[at],
            device_id=device,
            device_id_type=MESH,
        )
        copy.start()
        self.copies.append(copy)
        return copy

    def finish(self):
        for copy in self.copies:
            copy.wait_send()


def greet(devices):
    barrier = pltpu.get_barrier_semaphore()
    for device in devices:
        pl.semaphore_signal(barrier, inc=1, device_id=device, device_id_type=MESH)
    pl.semaphore_wait(barrier, len(devices))


def f32(values):
    return values.astype(jnp.float32)


def project(emb, weights, emb_v, w_v, acc, rows_v, landed, coords, core, meet, pass_on, local_sems, send, a2a_send, a2a_recv):
    dp, seq = lax.axis_index("dp"), lax.axis_index("seq")
    groups = lax.axis_size("seq")
    depth = weights.shape[0]
    partner = device_at(coords, 1 - core)
    sides = (device_at(moved(coords, 0, 1), core), device_at(moved(coords, 0, 3), core))
    across = lax.rem(dp + 2, 4)
    order = (dp, dp + 1 - 2 * core, across, across + 1 - 2 * core)
    own_w = pltpu.make_async_copy(weights, w_v.at[dp], local_sems.at[4])
    own_w.start()

    def load(at):
        cols = pl.ds(pl.multiple_of(order[at] * depth, depth), depth)
        copy = pltpu.make_async_copy(emb.at[:, cols], emb_v.at[at % 2], local_sems.at[at])
        copy.start()
        return copy

    loads = [load(0), load(1)]
    meet()

    def piece(stage, axis, owner, side):
        base, direct, size = STAGES[stage]
        start = base + direct + 4 * size * (axis - 1)
        if side is None:
            return pl.ds(pl.multiple_of(start + size * owner, 32), size)
        return pl.ds(pl.multiple_of(start + size * owner + size // 2 * side, 16), size // 2)

    def straight(stage, side):
        base, direct, _ = STAGES[stage]
        return pl.ds(base + direct // 2 * side, direct // 2)

    crossing, direct = {}, {}
    for stage in range(2):
        for axis in (1, 2):
            for side in range(2):
                rows = piece(stage, axis, coords[axis], side)
                crossing[stage, axis, side] = send(weights.at[rows], w_v.at[dp, rows], sides[side])
    for stage in range(2):
        for side in range(2):
            rows = straight(stage, side)
            direct[stage, side] = send(weights.at[rows], w_v.at[dp, rows], sides[side])
    to_partner = send(weights, w_v.at[dp], partner)

    def accumulate(at, row, size):
        acc[...] += jnp.dot(
            emb_v[at % 2, :, pl.ds(pl.multiple_of(row, 128), size)],
            w_v[order[at], pl.ds(pl.multiple_of(row, 128), size), :],
            preferred_element_type=jnp.float32,
        )

    rings, relays = {}, {}

    def spread(stage):
        for axis in (1, 2):
            for side in range(2):
                crossing[stage, axis, side].wait_recv()
                block = w_v.at[across, piece(stage, axis, coords[axis], side)]
                for k in (2, 1, 3):
                    rings.setdefault((stage, axis, k), []).append(
                        send(block, block, device_at(moved(coords, axis, k), core))
                    )

    def relay(stage, axis, k):
        block = w_v.at[across, piece(stage, axis, lax.rem(coords[axis] + 4 - k, 4), None)]
        relays[stage, axis, k] = send(block, block, partner)

    def collect(stage):
        for axis in (1, 2):
            relay(stage, axis, 0)
        for side in range(2):
            direct[stage, side].wait_recv()
            block = w_v.at[across, straight(stage, side)]
            relays[stage, 0, side] = send(block, block, partner)
        for k in (1, 3, 2):
            for axis in (1, 2):
                for copy in rings[stage, axis, k]:
                    copy.wait_recv()
                relay(stage, axis, k)

    def take(stage):
        for key, copy in relays.items():
            if key[0] == stage:
                copy.wait_recv()

    acc[...] = jnp.zeros_like(acc)
    loads[0].wait()
    own_w.wait()

    @pl.loop(0, depth // CHUNK)
    def _(step):
        accumulate(0, step * CHUNK, CHUNK)

    loads.append(load(2))
    spread(0)
    pass_on()
    loads[1].wait()
    to_partner.wait_recv()
    accumulate(1, 0, 1024)
    spread(1)
    accumulate(1, 1024, 1024)
    loads.append(load(3))
    loads[2].wait()
    collect(0)
    accumulate(2, 0, STAGE_ROWS[0])
    loads[3].wait()
    take(0)
    accumulate(3, 0, STAGE_ROWS[0])
    collect(1)
    accumulate(2, STAGE_ROWS[0], STAGE_ROWS[1])
    take(1)

    def block_copy(off):
        there = lax.rem(seq + off, groups)
        return pltpu.make_async_remote_copy(
            src_ref=rows_v.at[there],
            dst_ref=landed.at[seq],
            send_sem=a2a_send.at[off],
            recv_sem=a2a_recv.at[off],
            device_id=(dp, there),
            device_id_type=MESH,
        )

    tail = pl.ds(STAGE_ROWS[0], STAGE_ROWS[1])
    total = acc[...] + jnp.dot(emb_v[1, :, tail], w_v[order[3], tail, :], preferred_element_type=jnp.float32)
    rows_v[...] = total.astype(jnp.bfloat16).reshape(rows_v.shape)
    return block_copy


class Part:
    def __init__(self, order, terms, scratch, send, coords, core):
        self.order, self.terms, self.send, self.coords, self.core = order, terms, send, coords, core
        self.pair, self.halves, self.acc2, self.next, self.acc3, self.last = scratch
        self.acc1 = self.pair

    def start_pair(self):
        self.pair_copy = self.send(
            self.terms.at[1 - self.core], self.pair, device_at(self.coords, 1 - self.core)
        )

    def start_first(self):
        self.pair_copy.wait_recv()

        @pl.loop(0, 4)
        def _(at):
            self.acc1[at] = (f32(self.terms[self.core, at]) + f32(self.pair[at])).astype(jnp.bfloat16)

        acc, halves = self.acc1, self.halves
        here = self.coords[self.order[0]]
        self.up, self.down = (device_at(moved(self.coords, self.order[0], k), self.core) for k in (1, 3))
        after, before, opposite = (lax.rem(here + k, 4) for k in (1, 3, 2))
        low, high = pl.ds(0, 2), pl.ds(2, 2)
        self.arrivals = [
            self.send(acc.at[opposite, low], halves.at[0], self.up),
            self.send(acc.at[opposite, high], halves.at[1], self.down),
            self.send(acc.at[before, low], halves.at[2], self.down),
            self.send(acc.at[after, high], halves.at[3], self.up),
        ]

    def relay_first(self):
        acc, halves, here = self.acc1, self.halves, self.coords[self.order[0]]
        after, before = (lax.rem(here + k, 4) for k in (1, 3))
        self.arrivals[0].wait_recv()
        acc[after, 0:2] = (f32(halves[0]) + f32(acc[after, 0:2])).astype(jnp.bfloat16)
        self.arrivals.append(self.send(acc.at[after, pl.ds(0, 2)], halves.at[4], self.up))
        self.arrivals[1].wait_recv()
        acc[before, 2:4] = (f32(halves[1]) + f32(acc[before, 2:4])).astype(jnp.bfloat16)
        self.arrivals.append(self.send(acc.at[before, pl.ds(2, 2)], halves.at[5], self.down))

    def end_first(self):
        acc, halves, here = self.acc1, self.halves, self.coords[self.order[0]]
        for copy in self.arrivals[2:]:
            copy.wait_recv()
        self.acc2[0:2] = (f32(acc[here, 0:2]) + f32(halves[2]) + f32(halves[4])).astype(jnp.bfloat16)
        self.acc2[2:4] = (f32(acc[here, 2:4]) + f32(halves[3]) + f32(halves[5])).astype(jnp.bfloat16)
        self.exchange(1, self.acc2, self.next)

    def exchange(self, number, acc, into):
        axis = self.order[number]
        here = self.coords[axis]
        self.arrivals = [
            self.send(
                acc.at[lax.rem(here + k, 4)],
                into.at[k - 1],
                device_at(moved(self.coords, axis, k), self.core),
            )
            for k in (2, 1, 3)
        ]

    def gathered(self, number, acc, into):
        for copy in self.arrivals:
            copy.wait_recv()
        here = self.coords[self.order[number]]
        return (f32(acc[here]) + f32(into[0])) + (f32(into[1]) + f32(into[2]))

    def end_second(self):
        self.acc3[...] = self.gathered(1, self.acc2, self.next).astype(jnp.bfloat16)
        self.exchange(2, self.acc3, self.last)

    def end_last(self):
        return self.gathered(2, self.acc3, self.last)


def part_scratch(width):
    unit = (24, width)
    return [
        pltpu.VMEM(shape + unit, jnp.bfloat16)
        for shape in ((4, 4, 4), (6, 2, 4), (4, 4), (3, 4), (4,), (3,))
    ]


def gelu(values):
    return 0.5 * values * (1.0 + lax.erf(values * (1.0 / math.sqrt(2.0))))


def gelu_slope(values):
    cumulative = 0.5 * (1.0 + lax.erf(values * (1.0 / math.sqrt(2.0))))
    density = jnp.exp(-0.5 * values * values) * (1.0 / math.sqrt(2.0 * math.pi))
    return cumulative + values * density


def bf(values):
    return values.astype(jnp.bfloat16)


def dot(left, right):
    return jnp.dot(left, right, preferred_element_type=jnp.float32)


def dot_nt(left, right):
    return lax.dot_general(
        left, right, (((1,), (1,)), ((), ())), preferred_element_type=jnp.float32
    )


def flat(values):
    return values.reshape(-1, values.shape[-1])


def row_blocks(count, step, body):
    @pl.loop(0, count // step)
    def _(at):
        body(pl.multiple_of(at * step, step))


STEP = 16
HALF = 64
INNER = 384
CH = 768


def conv_forward(act, kernel, inner, edge_out, edge_in, send, after, before, seq, groups):
    low, high = flat(act[:, 0:HALF, :]), flat(act[:, HALF:128, :])
    shape = (act.shape[0], HALF, INNER)
    edge_out[0] = bf(dot(high, kernel[0])).reshape(shape)
    from_before = send(edge_out.at[0], edge_in.at[0], after)
    edge_out[1] = bf(dot(low, kernel[2])).reshape(shape)
    from_after = send(edge_out.at[1], edge_in.at[1], before)
    inner[:, 0:HALF, :] = (dot(low, kernel[1]) + dot(high, kernel[2])).reshape(shape)
    inner[:, HALF:128, :] = (dot(high, kernel[1]) + dot(low, kernel[0])).reshape(shape)
    return from_before, from_after


def finish_inner(inner, gated, edge_in, copies, seq, groups):
    copies[0].wait_recv()
    copies[1].wait_recv()
    keeps = (jnp.where(seq == 0, 0.0, 1.0), jnp.where(seq == groups - 1, 0.0, 1.0))
    for side in range(2):

        @pl.loop(0, inner.shape[0])
        def _(group):
            for row in range(0, HALF, STEP):
                rows = slice(side * HALF + row, side * HALF + row + STEP)
                total = inner[group, rows, :] + f32(edge_in[side, group, row : row + STEP, :]) * keeps[side]
                inner[group, rows, :] = total
                gated[group, rows, :] = bf(gelu(total))


def exchange_grads(wide, send, after, before):
    from_after = send(wide.at[1, :, pl.ds(0, HALF)], wide.at[0, :, pl.ds(HALF, HALF)], before)
    from_before = send(wide.at[1, :, pl.ds(HALF, HALF)], wide.at[2, :, pl.ds(0, HALF)], after)
    wide[0, :, 0:HALF, :] = wide[1, :, HALF:128, :]
    wide[2, :, HALF:128, :] = wide[1, :, 0:HALF, :]
    return from_after, from_before


def finish_exchange(wide, copies, seq, groups):
    copies[0].wait_recv()
    copies[1].wait_recv()
    zeros = jnp.zeros((wide.shape[1], HALF, INNER), jnp.bfloat16)

    @pl.when(seq == groups - 1)
    def _():
        wide[0, :, HALF:128, :] = zeros

    @pl.when(seq == 0)
    def _():
        wide[2, :, 0:HALF, :] = zeros


def gradient_rows(transposed, right, store):
    @pl.loop(0, 4)
    def _(y):
        result = dot(transposed[pl.ds(pl.multiple_of(y * 192, 64), 192), :], right())
        for x_hi in range(2):
            for z in range(4):
                row = 24 * (4 * x_hi + z)
                store(y, x_hi, z, bf(result[row : row + 24]))


def step_kernel(
    emb, weights, lane_position, length_ref, targets, kernels, mixers, readout,
    joined_out, readout_out, woven,
    emb_v, w_v, total, rows_v, landed, load_sems, a2a_send, a2a_recv, ready,
    kernels_v, mixers_v, readout_v, targets_v, local_sems,
    hid, act1, inner1, gated1, mixed, first, act2, inner2, gated2, second, logits, logit_grad,
    upper, wide2, wide1, lower, act1_t, act2_t, second_t, mixer_left, mixer_right,
    edge1_out, edge1_in, edge2_out, edge2_in, *rest
):
    terms, parts_scratch, (joined, send_sems, recv_sems) = rest[:N_PARTS], rest[N_PARTS:-3], rest[-3:]
    coords, core = place()
    dp, seq = lax.axis_index("dp"), lax.axis_index("seq")
    groups = lax.axis_size("seq")
    loads = []
    for at, (src, dst) in enumerate(
        (
            (kernels.at[0], kernels_v.at[0]),
            (mixers, mixers_v),
            (kernels.at[1], kernels_v.at[1]),
            (readout, readout_v),
            (targets, targets_v),
        )
    ):
        loads.append(pltpu.make_async_copy(src, dst, local_sems.at[at]))
    after, before = (dp, lax.rem(seq + 1, groups)), (dp, lax.rem(seq + groups - 1, groups))
    send = Sender(send_sems, recv_sems)
    parts = []
    for members in GROUPS:
        parts.append([])
        for order, _ in members:
            at = sum(len(group) for group in parts)
            parts[-1].append(Part(order, terms[at], parts_scratch[6 * at : 6 * at + 6], send, coords, core))

    def put(number, unit):
        def store(y, x_hi, z, block):
            spot = (2 * x_hi + unit // 2, y, z)
            start = 0
            for part, (order, width) in zip(parts[number], GROUPS[number]):
                part.terms[unit % 2, spot[order[0]], spot[order[1]], spot[order[2]]] = block[:, start : start + width]
                start += width

        return store

    def each(number, step):
        return [getattr(part, step)() for part in parts[number]]

    def gather_last(number):
        return jnp.concatenate(each(number, "end_last"), axis=1)

    pair_x = (coords[0] + 1 - 2 * lax.rem(coords[0], 2),) + coords[1:]
    partner = device_at(coords, 1 - core)
    group = [partner, device_at(pair_x, core), device_at(pair_x, 1 - core)]

    def meet():
        greet(
            [device_at(moved(coords, axis, k), core) for axis in range(3) for k in (1, 2, 3)]
            + [partner, device_at(pair_x, 1 - core), after, before]
        )
        for k in (1, 2, 3):
            pl.semaphore_signal(
                ready.at[0], inc=1, device_id=device_at(moved(coords, 1, k), core), device_id_type=MESH
            )

    def pass_on():
        for copy in loads:
            copy.start()
        pl.semaphore_wait(ready.at[0], 3)
        pl.semaphore_signal(
            ready.at[1], inc=1, device_id=device_at(moved(coords, 0, 2), core), device_id_type=MESH
        )

    block_copy = project(
        emb, weights, emb_v, w_v, total, rows_v, landed, coords, core, meet, pass_on, load_sems, send, a2a_send, a2a_recv
    )
    length = length_ref[0]

    pl.semaphore_wait(ready.at[1], 1)

    @pl.loop(1, groups)
    def _(off):
        block_copy(off).start()

    landed[seq] = rows_v[seq]

    @pl.loop(1, groups)
    def _(off):
        block_copy(off).wait()

    blocks = flat(landed[...])
    for group_at in range(4):
        spot = 4 * lax.broadcasted_iota(jnp.int32, (128, 512), 0) + group_at
        chosen = (lane_position[...] == spot) & (spot + seq * 512 < length)
        hid[group_at] = bf(dot(jnp.where(chosen, 1.0, 0.0).astype(jnp.bfloat16), blocks))

    for group_at in range(4):

        def gelu_rows(row, group_at=group_at):
            act1[group_at, pl.ds(row, STEP), :] = bf(gelu(f32(hid[group_at, pl.ds(row, STEP), :])))

        row_blocks(128, STEP, gelu_rows)

    loads[0].wait()
    edges = conv_forward(act1, kernels_v.at[0], inner1, edge1_out, edge1_in, send, after, before, seq, groups)
    act1_t[...] = flat(act1[...]).T
    finish_inner(inner1, gated1, edge1_in, edges, seq, groups)
    loads[1].wait()
    mixed[...] = dot(flat(gated1[...]), mixers_v[0]).reshape(mixed.shape)
    for pair in range(2):

        def pool_rows(row, pair=pair):
            rows = pl.ds(row, STEP)
            total = (f32(hid[2 * pair, rows, :]) + mixed[2 * pair, rows, :]) + (
                f32(hid[2 * pair + 1, rows, :]) + mixed[2 * pair + 1, rows, :]
            )
            pooled = bf(total * 0.5)
            first[pair, rows, :] = pooled
            act2[pair, rows, :] = bf(gelu(f32(pooled)))

        row_blocks(128, STEP, pool_rows)

    loads[2].wait()
    edges = conv_forward(act2, kernels_v.at[1], inner2, edge2_out, edge2_in, send, after, before, seq, groups)
    act2_t[...] = flat(act2[...]).T
    finish_inner(inner2, gated2, edge2_in, edges, seq, groups)
    mixed[0:2] = dot(flat(gated2[...]), mixers_v[1]).reshape(2, 128, CH)

    def pool_again(row):
        rows = pl.ds(row, STEP)
        total = (f32(first[0, rows, :]) + mixed[0, rows, :]) + (f32(first[1, rows, :]) + mixed[1, rows, :])
        second[rows, :] = bf(total * 0.5)

    row_blocks(128, STEP, pool_again)
    loads[3].wait()
    loads[4].wait()
    logits[...] = dot(second[...], readout_v[...])
    loss_scale = 2.0 / math.sqrt(lax.axis_size("dp") * groups * 128)

    def loss_rows(row):
        rows = pl.ds(row, 8)
        values = logits[rows, :]
        small = jnp.exp(-jnp.abs(values))
        softplus = jnp.maximum(values, 0.0) + jnp.log1p(small)
        sigmoid = jnp.where(values >= 0.0, 1.0, small) / (1.0 + small)
        bins = seq * 128 + row + lax.broadcasted_iota(jnp.int32, (8, 1), 0)
        valid = jnp.where(bins * 4 < length, loss_scale, 0.0)
        mixed_rows = valid * (softplus - targets_v[rows, :].astype(jnp.float32)) * sigmoid
        logits[rows, :] = mixed_rows

    row_blocks(128, 8, loss_rows)
    logit_grad[...] = bf(logits[...])
    second_t[...] = second[...].T
    for index in range(4):
        gradient_rows(second_t, lambda i=index: logit_grad[:, 512 * i : 512 * i + 512], put(2, index))
    each(2, "start_pair")

    upper[...] = bf(dot_nt(logit_grad[...], readout_v[...]) * 0.5)
    back = dot_nt(upper[...], mixers_v[1])
    logits[:, 0:INNER] = back

    def coarse_rows(row):
        rows = pl.ds(row, STEP)
        back_rows = logits[rows, 0:INNER]
        for pair in range(2):
            wide2[1, pair, rows, :] = bf(back_rows * gelu_slope(inner2[pair, rows, :]))

    row_blocks(128, STEP, coarse_rows)
    edges = exchange_grads(wide2, send, after, before)
    each(2, "start_first")
    gradient_rows(act2_t, lambda: flat(wide2[1]), put(1, 1))
    row_at = lax.broadcasted_iota(jnp.int32, (CH, INNER), 0)
    column = lax.broadcasted_iota(jnp.int32, (CH, INNER), 1)
    target_row = column + 12 * lax.shift_right_logical(column * 43691, 19)
    for half in range(2):
        picks = jnp.where(row_at == target_row + 12 * half, 1.0, 0.0).astype(jnp.bfloat16)
        mixer_left[:, 256 * half : 256 * half + 256] = bf(dot_nt(picks, flat(gated2[...])))
        for pair in range(2):
            row = 256 * half + 128 * pair
            mixer_right[row : row + 128] = upper[:, INNER * half : INNER * half + INNER]
    gradient_rows(mixer_left.at[:, pl.ds(0, 512)], lambda: mixer_right[0:512], put(1, 3))
    finish_exchange(wide2, edges, seq, groups)
    gradient_rows(act2_t, lambda: flat(wide2[0]), put(1, 0))
    gradient_rows(act2_t, lambda: flat(wide2[2]), put(1, 2))
    each(1, "start_pair")
    mixed[0:2] = (
        dot_nt(flat(wide2[0]), kernels_v[1, 0])
        + dot_nt(flat(wide2[1]), kernels_v[1, 1])
        + dot_nt(flat(wide2[2]), kernels_v[1, 2])
    ).reshape(2, 128, CH)
    trunk_scale = math.sqrt(lax.axis_size("dp") * groups * 128) * 0.5

    def trunk_rows(row):
        rows = pl.ds(row, STEP)
        upper_rows = f32(upper[rows, :])
        for pair in range(2):
            grad = upper_rows + mixed[pair, rows, :] * gelu_slope(f32(first[pair, rows, :]))
            scaled = grad * trunk_scale
            for at in range(6):
                woven[at, pl.ds(2 * row + pair, STEP, stride=2), :] = scaled[:, 128 * at : 128 * at + 128]
            lower[pair, rows, :] = bf(grad * 0.5)

    row_blocks(128, STEP, trunk_rows)
    each(2, "relay_first")
    each(1, "start_first")
    back = dot_nt(flat(lower[...]), mixers_v[0])
    mixed[0:2, :, 0:INNER] = back.reshape(2, 128, INNER)
    for pair in range(2):

        def fine_rows(row, pair=pair):
            rows = pl.ds(row, STEP)
            back_rows = mixed[pair, rows, 0:INNER]
            for side in range(2):
                wide1[1, 2 * pair + side, rows, :] = bf(back_rows * gelu_slope(inner1[2 * pair + side, rows, :]))

        row_blocks(128, STEP, fine_rows)

    edges = exchange_grads(wide1, send, after, before)
    each(2, "end_first")
    each(1, "relay_first")
    gradient_rows(act1_t, lambda: flat(wide1[1]), put(0, 1))
    for half in range(2):
        picks = jnp.where(row_at == target_row + 12 * half, 1.0, 0.0).astype(jnp.bfloat16)
        mixer_left[:, 512 * half : 512 * half + 512] = bf(dot_nt(picks, flat(gated1[...])))
        for group_at in range(4):
            row = 512 * half + 128 * group_at
            mixer_right[row : row + 128] = lower[group_at // 2, :, INNER * half : INNER * half + INNER]
    gradient_rows(mixer_left, lambda: mixer_right[...], put(0, 3))
    each(1, "end_first")
    finish_exchange(wide1, edges, seq, groups)
    gradient_rows(act1_t, lambda: flat(wide1[0]), put(0, 0))
    gradient_rows(act1_t, lambda: flat(wide1[2]), put(0, 2))
    each(0, "start_pair")
    each(2, "end_second")
    each(1, "end_second")
    each(0, "start_first")
    readout_out[...] = gather_last(2)
    each(0, "relay_first")
    joined[dp, :, 384:768] = gather_last(1)
    each(0, "end_first")
    each(0, "end_second")
    joined[dp, :, 0:384] = gather_last(0)
    mine = joined.at[dp]
    last = [send(mine, mine, device) for device in group]
    for copy in last:
        copy.wait_recv()
    joined_out[...] = joined[...]
    send.finish()


N_PARTS = sum(len(group) for group in GROUPS)
N_GATHER = 8 + 4 + 1 + 24 + 16 + 4
N_COPIES = N_GATHER + N_PARTS * (1 + 6 + 3 + 3) + 3 + 8


def finish_kernel(joined, readout_part, woven, kernel_out, mixer_out, readout_out, trunk_out):
    dp = lax.axis_index("dp")
    for index in range(4):

        @pl.when(dp == index)
        def _():
            low = 96 * index
            for tap in range(6):
                start = 384 * (tap // 3) + low
                kernel_out[tap // 3, tap % 3] = joined[tap % 3, :, start : start + 96]
            row, low = 12 * (index // 2), 192 * (index % 2)
            for block in range(2):
                start = 384 * block + low
                mixer_out[block] = joined[3, row : row + 12, start : start + 192]

    readout_out[...] = readout_part[...]
    for at in range(6):
        trunk_out[:, 128 * at : 128 * at + 128] = woven[at]


def write_outputs(joined, readout_part, woven):
    vmem, single = pl.BlockSpec(memory_space=pltpu.VMEM), jnp.float32
    return pl.pallas_call(
        finish_kernel,
        out_shape=(
            jax.ShapeDtypeStruct((2, 3, 24, 96), single),
            jax.ShapeDtypeStruct((2, 12, 192), single),
            jax.ShapeDtypeStruct((24, 512), single),
            jax.ShapeDtypeStruct((256, CH), single),
        ),
        in_specs=[vmem] * 3,
        out_specs=[vmem] * 4,
        name="outputs",
    )(joined, readout_part, woven)


def step(emb, weights, lane_position, length, targets, kernels, mixers, readout):
    vmem, anywhere = pl.BlockSpec(memory_space=pltpu.VMEM), pl.BlockSpec(memory_space=pl.ANY)
    bf16, single = jnp.bfloat16, jnp.float32
    rows, depth, groups = emb.shape[0], weights.shape[0], lax.axis_size("seq")
    blocks = (groups, rows // groups, CH)
    return pl.pallas_call(
        step_kernel,
        out_shape=(
            jax.ShapeDtypeStruct((4, 24, CH), single),
            jax.ShapeDtypeStruct((24, 512), single),
            jax.ShapeDtypeStruct((6, 256, 128), single),
        ),
        in_specs=[anywhere, anywhere, vmem, pl.BlockSpec(memory_space=pltpu.SMEM)] + [anywhere] * 4,
        out_specs=[vmem] * 3,
        scratch_shapes=[
            pltpu.VMEM((2, rows, depth), bf16),
            pltpu.VMEM((4, depth, CH), bf16),
            pltpu.VMEM((rows, CH), single),
            pltpu.VMEM(blocks, bf16),
            pltpu.VMEM(blocks, bf16),
            pltpu.SemaphoreType.DMA((5,)),
            pltpu.SemaphoreType.DMA((groups,)),
            pltpu.SemaphoreType.DMA((groups,)),
            pltpu.SemaphoreType.REGULAR((2,)),
            pltpu.VMEM((2, 3, CH, INNER), bf16),
            pltpu.VMEM((2, INNER, CH), bf16),
            pltpu.VMEM((CH, 2048), bf16),
            pltpu.VMEM((128, 2048), jnp.int32),
            pltpu.SemaphoreType.DMA((5,)),
            pltpu.VMEM((4, 128, CH), bf16),
            pltpu.VMEM((4, 128, CH), bf16),
            pltpu.VMEM((4, 128, INNER), single),
            pltpu.VMEM((4, 128, INNER), bf16),
            pltpu.VMEM((4, 128, CH), single),
            pltpu.VMEM((2, 128, CH), bf16),
            pltpu.VMEM((2, 128, CH), bf16),
            pltpu.VMEM((2, 128, INNER), single),
            pltpu.VMEM((2, 128, INNER), bf16),
            pltpu.VMEM((128, CH), bf16),
            pltpu.VMEM((128, 2048), single),
            pltpu.VMEM((128, 2048), bf16),
            pltpu.VMEM((128, CH), bf16),
            pltpu.VMEM((3, 2, 128, INNER), bf16),
            pltpu.VMEM((3, 4, 128, INNER), bf16),
            pltpu.VMEM((2, 128, CH), bf16),
            pltpu.VMEM((CH, 512), bf16),
            pltpu.VMEM((CH, 256), bf16),
            pltpu.VMEM((CH, 128), bf16),
            pltpu.VMEM((CH, 1024), bf16),
            pltpu.VMEM((1024, INNER), bf16),
            pltpu.VMEM((2, 4, HALF, INNER), bf16),
            pltpu.VMEM((2, 4, HALF, INNER), bf16),
            pltpu.VMEM((2, 2, HALF, INNER), bf16),
            pltpu.VMEM((2, 2, HALF, INNER), bf16),
        ]
        + [pltpu.VMEM((2, 4, 4, 4, 24, width), bf16) for group in GROUPS for _, width in group]
        + [s for group in GROUPS for _, width in group for s in part_scratch(width)]
        + [
            pltpu.VMEM((4, 24, CH), single),
            pltpu.SemaphoreType.DMA((N_COPIES,)),
            pltpu.SemaphoreType.DMA((N_COPIES,)),
        ],
        compiler_params=pltpu.CompilerParams(
            collective_id=0, has_side_effects=True, vmem_limit_bytes=66 * 10**6
        ),
        name="step",
    )(emb, weights, lane_position, length, targets, kernels, mixers, readout)


def shards(embeddings, layout, lengths, targets, projection, kernels, mixers, readout):
    row_count = embeddings.shape[2]
    block_rows = row_count // lax.axis_size("seq")
    column = lax.dynamic_index_in_dim(layout[0], lax.axis_index("seq"), axis=1, keepdims=False)
    lane_position = (
        column[:, None] * block_rows + jnp.arange(block_rows, dtype=jnp.int32)[None, :]
    ).reshape(1, row_count)
    kernel_total, mixer_total, readout_total, trunk_grad = write_outputs(
        *step(embeddings[0, 0], projection, lane_position, lengths, targets[0], kernels, mixers, readout)
    )
    return (kernel_total, mixer_total, readout_total, trunk_grad[None])


def solution(mesh):
    placed = (
        P("dp", "seq", None, None),
        P("dp", None, None),
        P("dp"),
        P("dp", "seq", None),
        P("dp", None),
        P(),
        P(),
        P(),
    )
    return jax.shard_map(
        shards,
        mesh=mesh,
        in_specs=placed,
        out_specs=(
            P(None, None, "seq", "dp"),
            P(None, "seq", "dp"),
            P("seq", "dp"),
            P("dp", "seq", None),
        ),
        check_vma=False,
    )
```

profile of v0, /device:TPU:1, one launch (start us, length us, event | category | flops | bytes accessed | tf_op | source)
XLA Modules:
  0.0 130.4 jit_solution(3886808950437523363)
XLA Ops:
  1.3 0.9 multiply_reduce_fusion
  2.2 0.1 iota_add_fusion
  2.3 0.7 add.31.lane_position
  2.9 123.8 %step.1 = (f32[4,24,768]{2,1,0:T(8,128)}, f32[24,512]{1,0:T(8,128)}, f32[6,256,128]{2,1,0:T(8,128)}) custom-call(bf16[512,8192]{1,0:T(8,128)(2,1)} %bitcast.3, bf16[2048,768]{1,0:T(8,128)(2,1)} %weights.1, s32[1,512]{1,0:T(1,128)} %add.31.lane_position, s32[1]{0:T(128)S(6)} %copy.14.length_ref, s32[128,2048]{1,0:T(8,128)} %bitcast.4, ...), custom_call_target="tpu_custom_call" | custom-call | tf_op jit(solution)/shard_map/step/pallas_call | solution.py:676
  126.7 2.3 %outputs.1 = (f32[2,3,24,96]{3,2,1,0:T(8,128)}, f32[2,12,192]{2,1,0:T(8,128)}, f32[24,512]{1,0:T(8,128)}, f32[256,768]{1,0:T(8,128)}) custom-call(f32[4,24,768]{2,1,0:T(8,128)} %get-tuple-element.11.joined, f32[24,512]{1,0:T(8,128)} %get-tuple-element.12.readout_part, f32[6,256,128]{2,1,0:T(8,128)} %get-tuple-element.13.woven), custom_call_target="tpu_custom_call" | custom-call | tf_op jit(solution)/shard_map/outputs/pallas_call | solution.py:657
  129.0 1.4 %copy.13 = f32[2,12,192]{2,0,1:T(2,128)} copy(f32[2,12,192]{2,1,0:T(8,128)} %get-tuple-element.23) | data formatting | bytes 36864
where the time goes:
time: 131 us; the launch traced here: 130 us
  Pallas kernels  126 us (96%)
  local copies, waits for them, and re-layouts  2.06 us (2%)
    pallas_call x1, Pallas kernels, step(): pl.pallas_call(step_kernel, out_shape=(jax.ShapeDtypeStruct((4, 24, CH),...  124 us

commit v1 on v0

--- a/solution.py
+++ b/solution.py
@@ -13,7 +13,7 @@
 STAGE_ROWS = (1280, 768)
 GROUPS = (
     (((0, 1, 2), 128), ((1, 2, 0), 128), ((2, 0, 1), 128)),
-    (((0, 1, 2), 128), ((1, 2, 0), 128), ((2, 0, 1), 128)),
+    (((0, 1, 2), 128), ((1, 0, 2), 256)),
     (((1, 0, 2), 256), ((0, 1, 2), 256)),
 )
 
@@ -214,7 +214,7 @@
 
         @pl.loop(0, 4)
         def _(at):
-            self.acc1[at] = (f32(self.terms[self.core, at]) + f32(self.pair[at])).astype(jnp.bfloat16)
+            self.acc1[at] = self.terms[self.core, at] + self.pair[at]
 
         acc, halves = self.acc1, self.halves
         here = self.coords[self.order[0]]
@@ -232,10 +232,10 @@
         acc, halves, here = self.acc1, self.halves, self.coords[self.order[0]]
         after, before = (lax.rem(here + k, 4) for k in (1, 3))
         self.arrivals[0].wait_recv()
-        acc[after, 0:2] = (f32(halves[0]) + f32(acc[after, 0:2])).astype(jnp.bfloat16)
+        acc[after, 0:2] = halves[0] + acc[after, 0:2]
         self.arrivals.append(self.send(acc.at[after, pl.ds(0, 2)], halves.at[4], self.up))
         self.arrivals[1].wait_recv()
-        acc[before, 2:4] = (f32(halves[1]) + f32(acc[before, 2:4])).astype(jnp.bfloat16)
+        acc[before, 2:4] = halves[1] + acc[before, 2:4]
         self.arrivals.append(self.send(acc.at[before, pl.ds(2, 2)], halves.at[5], self.down))
 
     def end_first(self):
@@ -380,12 +380,12 @@
 
 
 def step_kernel(
-    emb, weights, lane_position, length_ref, targets, kernels, mixers, readout,
-    joined_out, readout_out, woven,
-    emb_v, w_v, total, rows_v, landed, load_sems, a2a_send, a2a_recv, ready,
+    emb, weights, layout, length_ref, targets, kernels, mixers, readout,
+    joined_out, readout_out, woven_out,
+    layout_v, emb_v, w_v, total, rows_v, landed, load_sems, a2a_send, a2a_recv, ready,
     kernels_v, mixers_v, readout_v, targets_v, local_sems,
     hid, act1, inner1, gated1, mixed, first, act2, inner2, gated2, second, logits, logit_grad,
-    upper, wide2, wide1, lower, act1_t, act2_t, second_t, mixer_left, mixer_right,
+    upper, woven, wide2, wide1, lower, act1_t, act2_t, second_t, gated1_t, gated2_t, picks, mixer_right, mixer_grad,
     edge1_out, edge1_in, edge2_out, edge2_in, *rest
 ):
     terms, parts_scratch, (joined, send_sems, recv_sems) = rest[:N_PARTS], rest[N_PARTS:-3], rest[-3:]
@@ -400,6 +400,7 @@
             (kernels.at[1], kernels_v.at[1]),
             (readout, readout_v),
             (targets, targets_v),
+            (layout, layout_v),
         )
     ):
         loads.append(pltpu.make_async_copy(src, dst, local_sems.at[at]))
@@ -445,6 +446,12 @@
     def pass_on():
         for copy in loads:
             copy.start()
+        column = lax.broadcasted_iota(jnp.int32, (CH, CH), 1)
+        half = jnp.where(column >= INNER, 1, 0)
+        column = column - INNER * half
+        target_row = column + 12 * lax.shift_right_logical(column * 43691, 19) + 12 * half
+        owner = lax.broadcasted_iota(jnp.int32, (CH, CH), 0)
+        picks[...] = jnp.where(owner == target_row, 1.0, 0.0).astype(jnp.bfloat16)
         pl.semaphore_wait(ready.at[0], 3)
         pl.semaphore_signal(
             ready.at[1], inc=1, device_id=device_at(moved(coords, 0, 2), core), device_id_type=MESH
@@ -467,10 +474,18 @@
     def _(off):
         block_copy(off).wait()
 
+    loads[5].wait()
+    here = lax.broadcasted_iota(jnp.int32, (32, 32), 1) == seq
+    column = jnp.sum(jnp.where(here, f32(layout_v[...]), 0.0), axis=1, keepdims=True)
+    lane = lax.broadcasted_iota(jnp.int32, (32, 512), 1)
+    source = lax.broadcasted_iota(jnp.int32, (32, 512), 0) == lax.shift_right_logical(lane, 4)
+    slot = jnp.sum(jnp.where(source, column, 0.0), axis=0, keepdims=True)
+    lane_position = slot * 16.0 + f32(lane[0:1] & 15)
+
     blocks = flat(landed[...])
     for group_at in range(4):
         spot = 4 * lax.broadcasted_iota(jnp.int32, (128, 512), 0) + group_at
-        chosen = (lane_position[...] == spot) & (spot + seq * 512 < length)
+        chosen = (lane_position == f32(spot)) & (spot + seq * 512 < length)
         hid[group_at] = bf(dot(jnp.where(chosen, 1.0, 0.0).astype(jnp.bfloat16), blocks))
 
     for group_at in range(4):
@@ -502,6 +517,7 @@
     loads[2].wait()
     edges = conv_forward(act2, kernels_v.at[1], inner2, edge2_out, edge2_in, send, after, before, seq, groups)
     act2_t[...] = flat(act2[...]).T
+    gated1_t[...] = flat(gated1[...]).T
     finish_inner(inner2, gated2, edge2_in, edges, seq, groups)
     mixed[0:2] = dot(flat(gated2[...]), mixers_v[1]).reshape(2, 128, CH)
 
@@ -529,11 +545,6 @@
 
     row_blocks(128, 8, loss_rows)
     logit_grad[...] = bf(logits[...])
-    second_t[...] = second[...].T
-    for index in range(4):
-        gradient_rows(second_t, lambda i=index: logit_grad[:, 512 * i : 512 * i + 512], put(2, index))
-    each(2, "start_pair")
-
     upper[...] = bf(dot_nt(logit_grad[...], readout_v[...]) * 0.5)
     back = dot_nt(upper[...], mixers_v[1])
     logits[:, 0:INNER] = back
@@ -546,18 +557,23 @@
 
     row_blocks(128, STEP, coarse_rows)
     edges = exchange_grads(wide2, send, after, before)
+    second_t[...] = second[...].T
+    for index in range(4):
+        gradient_rows(second_t, lambda i=index: logit_grad[:, 512 * i : 512 * i + 512], put(2, index))
+    each(2, "start_pair")
+    gradient_rows(act2_t, lambda: flat(wide2[1]), put(1, 1))
+
+    def mixer_gradient(gated_t, right, store):
+        total = dot(gated_t[...], right)
+        mixer_grad[0:INNER] = bf(total[:, 0:INNER])
+        mixer_grad[INNER:CH] = bf(total[:, INNER:CH])
+        gradient_rows(picks, lambda: mixer_grad[...], store)
+
+    gated2_t[...] = flat(gated2[...]).T
+    for pair in range(2):
+        mixer_right[128 * pair : 128 * pair + 128] = upper[...]
+    mixer_gradient(gated2_t, mixer_right[0:256], put(1, 3))
     each(2, "start_first")
-    gradient_rows(act2_t, lambda: flat(wide2[1]), put(1, 1))
-    row_at = lax.broadcasted_iota(jnp.int32, (CH, INNER), 0)
-    column = lax.broadcasted_iota(jnp.int32, (CH, INNER), 1)
-    target_row = column + 12 * lax.shift_right_logical(column * 43691, 19)
-    for half in range(2):
-        picks = jnp.where(row_at == target_row + 12 * half, 1.0, 0.0).astype(jnp.bfloat16)
-        mixer_left[:, 256 * half : 256 * half + 256] = bf(dot_nt(picks, flat(gated2[...])))
-        for pair in range(2):
-            row = 256 * half + 128 * pair
-            mixer_right[row : row + 128] = upper[:, INNER * half : INNER * half + INNER]
-    gradient_rows(mixer_left.at[:, pl.ds(0, 512)], lambda: mixer_right[0:512], put(1, 3))
     finish_exchange(wide2, edges, seq, groups)
     gradient_rows(act2_t, lambda: flat(wide2[0]), put(1, 0))
     gradient_rows(act2_t, lambda: flat(wide2[2]), put(1, 2))
@@ -580,6 +596,8 @@
             lower[pair, rows, :] = bf(grad * 0.5)
 
     row_blocks(128, STEP, trunk_rows)
+    woven_copy = pltpu.make_async_copy(woven, woven_out, local_sems.at[6])
+    woven_copy.start()
     each(2, "relay_first")
     each(1, "start_first")
     back = dot_nt(flat(lower[...]), mixers_v[0])
@@ -598,13 +616,9 @@
     each(2, "end_first")
     each(1, "relay_first")
     gradient_rows(act1_t, lambda: flat(wide1[1]), put(0, 1))
-    for half in range(2):
-        picks = jnp.where(row_at == target_row + 12 * half, 1.0, 0.0).astype(jnp.bfloat16)
-        mixer_left[:, 512 * half : 512 * half + 512] = bf(dot_nt(picks, flat(gated1[...])))
-        for group_at in range(4):
-            row = 512 * half + 128 * group_at
-            mixer_right[row : row + 128] = lower[group_at // 2, :, INNER * half : INNER * half + INNER]
-    gradient_rows(mixer_left, lambda: mixer_right[...], put(0, 3))
+    for group_at in range(4):
+        mixer_right[128 * group_at : 128 * group_at + 128] = lower[group_at // 2]
+    mixer_gradient(gated1_t, mixer_right[...], put(0, 3))
     each(1, "end_first")
     finish_exchange(wide1, edges, seq, groups)
     gradient_rows(act1_t, lambda: flat(wide1[0]), put(0, 0))
@@ -623,6 +637,7 @@
     last = [send(mine, mine, device) for device in group]
     for copy in last:
         copy.wait_recv()
+    woven_copy.wait()
     joined_out[...] = joined[...]
     send.finish()
 
@@ -645,7 +660,7 @@
             row, low = 12 * (index // 2), 192 * (index % 2)
             for block in range(2):
                 start = 384 * block + low
-                mixer_out[block] = joined[3, row : row + 12, start : start + 192]
+                mixer_out[:, block, :] = joined[3, row : row + 12, start : start + 192]
 
     readout_out[...] = readout_part[...]
     for at in range(6):
@@ -658,7 +673,7 @@
         finish_kernel,
         out_shape=(
             jax.ShapeDtypeStruct((2, 3, 24, 96), single),
-            jax.ShapeDtypeStruct((2, 12, 192), single),
+            jax.ShapeDtypeStruct((12, 2, 192), single),
             jax.ShapeDtypeStruct((24, 512), single),
             jax.ShapeDtypeStruct((256, CH), single),
         ),
@@ -668,7 +683,7 @@
     )(joined, readout_part, woven)
 
 
-def step(emb, weights, lane_position, length, targets, kernels, mixers, readout):
+def step(emb, weights, layout, length, targets, kernels, mixers, readout):
     vmem, anywhere = pl.BlockSpec(memory_space=pltpu.VMEM), pl.BlockSpec(memory_space=pl.ANY)
     bf16, single = jnp.bfloat16, jnp.float32
     rows, depth, groups = emb.shape[0], weights.shape[0], lax.axis_size("seq")
@@ -680,9 +695,10 @@
             jax.ShapeDtypeStruct((24, 512), single),
             jax.ShapeDtypeStruct((6, 256, 128), single),
         ),
-        in_specs=[anywhere, anywhere, vmem, pl.BlockSpec(memory_space=pltpu.SMEM)] + [anywhere] * 4,
-        out_specs=[vmem] * 3,
+        in_specs=[anywhere] * 3 + [pl.BlockSpec(memory_space=pltpu.SMEM)] + [anywhere] * 4,
+        out_specs=[vmem, vmem, anywhere],
         scratch_shapes=[
+            pltpu.VMEM((groups, groups), jnp.int32),
             pltpu.VMEM((2, rows, depth), bf16),
             pltpu.VMEM((4, depth, CH), bf16),
             pltpu.VMEM((rows, CH), single),
@@ -696,7 +712,7 @@
             pltpu.VMEM((2, INNER, CH), bf16),
             pltpu.VMEM((CH, 2048), bf16),
             pltpu.VMEM((128, 2048), jnp.int32),
-            pltpu.SemaphoreType.DMA((5,)),
+            pltpu.SemaphoreType.DMA((7,)),
             pltpu.VMEM((4, 128, CH), bf16),
             pltpu.VMEM((4, 128, CH), bf16),
             pltpu.VMEM((4, 128, INNER), single),
@@ -710,14 +726,18 @@
             pltpu.VMEM((128, 2048), single),
             pltpu.VMEM((128, 2048), bf16),
             pltpu.VMEM((128, CH), bf16),
+            pltpu.VMEM((6, 256, 128), single),
             pltpu.VMEM((3, 2, 128, INNER), bf16),
             pltpu.VMEM((3, 4, 128, INNER), bf16),
             pltpu.VMEM((2, 128, CH), bf16),
             pltpu.VMEM((CH, 512), bf16),
             pltpu.VMEM((CH, 256), bf16),
             pltpu.VMEM((CH, 128), bf16),
-            pltpu.VMEM((CH, 1024), bf16),
-            pltpu.VMEM((1024, INNER), bf16),
+            pltpu.VMEM((INNER, 512), bf16),
+            pltpu.VMEM((INNER, 256), bf16),
+            pltpu.VMEM((CH, CH), bf16),
+            pltpu.VMEM((512, CH), bf16),
+            pltpu.VMEM((CH, INNER), bf16),
             pltpu.VMEM((2, 4, HALF, INNER), bf16),
             pltpu.VMEM((2, 4, HALF, INNER), bf16),
             pltpu.VMEM((2, 2, HALF, INNER), bf16),
@@ -734,20 +754,14 @@
             collective_id=0, has_side_effects=True, vmem_limit_bytes=66 * 10**6
         ),
         name="step",
-    )(emb, weights, lane_position, length, targets, kernels, mixers, readout)
+    )(emb, weights, layout, length, targets, kernels, mixers, readout)
 
 
 def shards(embeddings, layout, lengths, targets, projection, kernels, mixers, readout):
-    row_count = embeddings.shape[2]
-    block_rows = row_count // lax.axis_size("seq")
-    column = lax.dynamic_index_in_dim(layout[0], lax.axis_index("seq"), axis=1, keepdims=False)
-    lane_position = (
-        column[:, None] * block_rows + jnp.arange(block_rows, dtype=jnp.int32)[None, :]
-    ).reshape(1, row_count)
     kernel_total, mixer_total, readout_total, trunk_grad = write_outputs(
-        *step(embeddings[0, 0], projection, lane_position, lengths, targets[0], kernels, mixers, readout)
+        *step(embeddings[0, 0], projection, layout[0], lengths, targets[0], kernels, mixers, readout)
     )
-    return (kernel_total, mixer_total, readout_total, trunk_grad[None])
+    return (kernel_total, mixer_total.transpose(1, 0, 2), readout_total, trunk_grad[None])
 
 
 def solution(mesh):

time: 131 us -> 129 us (0.985)
  local copies, waits for them, and re-layouts: 2.06 us -> 0 us
    unnamed x1 -> x0, local copies, waits for them, and re-layouts: 1.38 us -> none
where the time goes in v1:
time: 129 us; the launch traced here: 128 us
  Pallas kernels  127 us (98%)
  between operations  1.29 us (1%)
    pallas_call x1, Pallas kernels, step(): pl.pallas_call(step_kernel, out_shape=(jax.ShapeDtypeStruct((4, 24, CH),...  125 us

profile of v1, /device:TPU:1, one launch (start us, length us, event | category | flops | bytes accessed | tf_op | source)
XLA Modules:
  0.0 128.4 jit_solution(8302910756937946194)
XLA Ops:
  1.3 124.8 %step.1 = (f32[4,24,768]{2,1,0:T(8,128)}, f32[24,512]{1,0:T(8,128)}, f32[6,256,128]{2,1,0:T(8,128)}) custom-call(bf16[512,8192]{1,0:T(8,128)(2,1)} %bitcast.5, bf16[2048,768]{1,0:T(8,128)(2,1)} %weights.1, s32[32,32]{1,0:T(8,128)} %bitcast.7, s32[1]{0:T(128)S(6)} %copy.12.length_ref, s32[128,2048]{1,0:T(8,128)} %bitcast.6, bf16[2,3,768,384]{3,2,1,0:T(8,128)(2,1)} %kernels.1, ...), custom_call_target="tpu_custom_call" | custom-call | tf_op jit(solution)/shard_map/step/pallas_call | solution.py:691
  126.0 2.3 %outputs.1 = (f32[2,3,24,96]{3,2,1,0:T(8,128)}, f32[12,2,192]{2,1,0:T(2,128)}, f32[24,512]{1,0:T(8,128)}, f32[256,768]{1,0:T(8,128)}) custom-call(f32[4,24,768]{2,1,0:T(8,128)} %get-tuple-element.11.joined, f32[24,512]{1,0:T(8,128)} %get-tuple-element.12.readout_part, f32[6,256,128]{2,1,0:T(8,128)} %get-tuple-element.13.woven), custom_call_target="tpu_custom_call" | custom-call | tf_op jit(solution)/shard_map/outputs/pallas_call | solution.py:672

commit v2 on v1

--- a/solution.py
+++ b/solution.py
@@ -13,7 +13,7 @@
 STAGE_ROWS = (1280, 768)
 GROUPS = (
     (((0, 1, 2), 128), ((1, 2, 0), 128), ((2, 0, 1), 128)),
-    (((0, 1, 2), 128), ((1, 0, 2), 256)),
+    (((0, 1, 2), 128), ((1, 2, 0), 128), ((2, 0, 1), 128)),
     (((1, 0, 2), 256), ((0, 1, 2), 256)),
 )
 
@@ -272,11 +272,49 @@
         return self.gathered(2, self.acc3, self.last)
 
 
-def part_scratch(width):
+class TailPart(Part):
+    def exchange(self, number, acc, into):
+        if number < 2:
+            return Part.exchange(self, number, acc, into)
+        axis, (x, y, z), core = self.order[2], self.coords, self.core
+        x_hi, x_lo = lax.div(x, 2), lax.rem(x, 2)
+        self.arrivals = []
+        for other_lo in range(2):
+            there_lo = x_lo if other_lo == 0 else 1 - x_lo
+            for other_core in range(2):
+                there_core = core if other_core == 0 else 1 - core
+                for k in range(2 if axis == 0 else 4):
+                    if other_lo + other_core + k == 0:
+                        continue
+                    if axis == 0:
+                        there_hi = x_hi if k == 0 else 1 - x_hi
+                        block = acc.at[pl.ds(2 * there_hi, 2)]
+                        slot, device = into.at[x, core], device_at((2 * there_hi + there_lo, y, z), there_core)
+                    else:
+                        coords = moved((2 * x_hi + there_lo, y, z), axis, k)
+                        block = acc.at[coords[axis]]
+                        slot = into.at[self.coords[axis], x_lo, core]
+                        device = device_at(coords, there_core)
+                    self.arrivals.append(self.send(block, slot, device))
+        if axis == 0:
+            into[x, core] = acc[pl.ds(2 * x_hi, 2)]
+        else:
+            here = self.coords[axis]
+            into[here, x_lo, core] = acc[here]
+
+    def units(self):
+        for copy in self.arrivals:
+            copy.wait_recv()
+        if self.order[2] == 0:
+            return [sum(f32(self.last[x, core, lo]) for x in range(4)) for lo in range(2) for core in range(2)]
+        return [sum(f32(self.last[at, lo, core]) for at in range(4)) for lo in range(2) for core in range(2)]
+
+
+def part_scratch(width, tail):
     unit = (24, width)
     return [
         pltpu.VMEM(shape + unit, jnp.bfloat16)
-        for shape in ((4, 4, 4), (6, 2, 4), (4, 4), (3, 4), (4,), (3,))
+        for shape in ((4, 4, 4), (6, 2, 4), (4, 4), (3, 4), (4,), (4, 2, 2) if tail else (3,))
     ]
 
 
@@ -411,7 +449,8 @@
         parts.append([])
         for order, _ in members:
             at = sum(len(group) for group in parts)
-            parts[-1].append(Part(order, terms[at], parts_scratch[6 * at : 6 * at + 6], send, coords, core))
+            kind = TailPart if len(parts) == 1 else Part
+            parts[-1].append(kind(order, terms[at], parts_scratch[6 * at : 6 * at + 6], send, coords, core))
 
     def put(number, unit):
         def store(y, x_hi, z, block):
@@ -573,8 +612,8 @@
     for pair in range(2):
         mixer_right[128 * pair : 128 * pair + 128] = upper[...]
     mixer_gradient(gated2_t, mixer_right[0:256], put(1, 3))
+    finish_exchange(wide2, edges, seq, groups)
     each(2, "start_first")
-    finish_exchange(wide2, edges, seq, groups)
     gradient_rows(act2_t, lambda: flat(wide2[0]), put(1, 0))
     gradient_rows(act2_t, lambda: flat(wide2[2]), put(1, 2))
     each(1, "start_pair")
@@ -583,6 +622,8 @@
         + dot_nt(flat(wide2[1]), kernels_v[1, 1])
         + dot_nt(flat(wide2[2]), kernels_v[1, 2])
     ).reshape(2, 128, CH)
+    each(1, "start_first")
+    each(2, "relay_first")
     trunk_scale = math.sqrt(lax.axis_size("dp") * groups * 128) * 0.5
 
     def trunk_rows(row):
@@ -590,16 +631,11 @@
         upper_rows = f32(upper[rows, :])
         for pair in range(2):
             grad = upper_rows + mixed[pair, rows, :] * gelu_slope(f32(first[pair, rows, :]))
-            scaled = grad * trunk_scale
-            for at in range(6):
-                woven[at, pl.ds(2 * row + pair, STEP, stride=2), :] = scaled[:, 128 * at : 128 * at + 128]
+            mixed[2 + pair, rows, :] = grad * trunk_scale
             lower[pair, rows, :] = bf(grad * 0.5)
 
     row_blocks(128, STEP, trunk_rows)
-    woven_copy = pltpu.make_async_copy(woven, woven_out, local_sems.at[6])
-    woven_copy.start()
-    each(2, "relay_first")
-    each(1, "start_first")
+    each(1, "relay_first")
     back = dot_nt(flat(lower[...]), mixers_v[0])
     mixed[0:2, :, 0:INNER] = back.reshape(2, 128, INNER)
     for pair in range(2):
@@ -614,12 +650,22 @@
 
     edges = exchange_grads(wide1, send, after, before)
     each(2, "end_first")
-    each(1, "relay_first")
     gradient_rows(act1_t, lambda: flat(wide1[1]), put(0, 1))
+    each(1, "end_first")
     for group_at in range(4):
         mixer_right[128 * group_at : 128 * group_at + 128] = lower[group_at // 2]
     mixer_gradient(gated1_t, mixer_right[...], put(0, 3))
-    each(1, "end_first")
+
+    def weave_rows(row):
+        for pair in range(2):
+            for at in range(6):
+                woven[at, pl.ds(2 * row + pair, STEP, stride=2), :] = mixed[
+                    2 + pair, pl.ds(row, STEP), 128 * at : 128 * at + 128
+                ]
+
+    row_blocks(128, STEP, weave_rows)
+    woven_copy = pltpu.make_async_copy(woven, woven_out, local_sems.at[6])
+    woven_copy.start()
     finish_exchange(wide1, edges, seq, groups)
     gradient_rows(act1_t, lambda: flat(wide1[0]), put(0, 0))
     gradient_rows(act1_t, lambda: flat(wide1[2]), put(0, 2))
@@ -630,11 +676,13 @@
     readout_out[...] = gather_last(2)
     each(0, "relay_first")
     joined[dp, :, 384:768] = gather_last(1)
+    mine = joined.at[dp, :, pl.ds(384, 384)]
+    last = [send(mine, mine, device) for device in group]
     each(0, "end_first")
     each(0, "end_second")
-    joined[dp, :, 0:384] = gather_last(0)
-    mine = joined.at[dp]
-    last = [send(mine, mine, device) for device in group]
+    for at, part in enumerate(parts[0]):
+        for unit, values in enumerate(part.units()):
+            joined[unit, :, 128 * at : 128 * at + 128] = values
     for copy in last:
         copy.wait_recv()
     woven_copy.wait()
@@ -644,7 +692,7 @@
 
 N_PARTS = sum(len(group) for group in GROUPS)
 N_GATHER = 8 + 4 + 1 + 24 + 16 + 4
-N_COPIES = N_GATHER + N_PARTS * (1 + 6 + 3 + 3) + 3 + 8
+N_COPIES = N_GATHER + N_PARTS * (1 + 6 + 3 + 3) + (12 + 12 + 4) + 3 + 8
 
 
 def finish_kernel(joined, readout_part, woven, kernel_out, mixer_out, readout_out, trunk_out):
@@ -744,7 +792,7 @@
             pltpu.VMEM((2, 2, HALF, INNER), bf16),
         ]
         + [pltpu.VMEM((2, 4, 4, 4, 24, width), bf16) for group in GROUPS for _, width in group]
-        + [s for group in GROUPS for _, width in group for s in part_scratch(width)]
+        + [s for at, group in enumerate(GROUPS) for _, width in group for s in part_scratch(width, at == 0)]
         + [
             pltpu.VMEM((4, 24, CH), single),
             pltpu.SemaphoreType.DMA((N_COPIES,)),

time: 129 us -> 124 us (0.961)
  Pallas kernels: 127 us -> 123 us
    pallas_call x1, Pallas kernels: 125 us -> 121 us  [step(): pl.pallas_call(step_kernel, out_shape=(jax.ShapeDtypeStruct((4, 24, CH),...]
where the time goes in v2:
time: 124 us
  Pallas kernels  123 us (99%)
  between operations  1.29 us (1%)
    pallas_call x1, Pallas kernels, step(): pl.pallas_call(step_kernel, out_shape=(jax.ShapeDtypeStruct((4, 24, CH),...  121 us

profile of v2, /device:TPU:1, one launch (start us, length us, event | category | flops | bytes accessed | tf_op | source)
XLA Modules:
  0.0 124.3 jit_solution(6040536256738530604)
XLA Ops:
  1.3 120.7 %step.1 = (f32[4,24,768]{2,1,0:T(8,128)}, f32[24,512]{1,0:T(8,128)}, f32[6,256,128]{2,1,0:T(8,128)}) custom-call(bf16[512,8192]{1,0:T(8,128)(2,1)} %bitcast.5, bf16[2048,768]{1,0:T(8,128)(2,1)} %weights.1, s32[32,32]{1,0:T(8,128)} %bitcast.7, s32[1]{0:T(128)S(6)} %copy.12.length_ref, s32[128,2048]{1,0:T(8,128)} %bitcast.6, bf16[2,3,768,384]{3,2,1,0:T(8,128)(2,1)} %kernels.1, ...), custom_call_target="tpu_custom_call" | custom-call | tf_op jit(solution)/shard_map/step/pallas_call | solution.py:739
  122.0 2.3 %outputs.1 = (f32[2,3,24,96]{3,2,1,0:T(8,128)}, f32[12,2,192]{2,1,0:T(2,128)}, f32[24,512]{1,0:T(8,128)}, f32[256,768]{1,0:T(8,128)}) custom-call(f32[4,24,768]{2,1,0:T(8,128)} %get-tuple-element.11.joined, f32[24,512]{1,0:T(8,128)} %get-tuple-element.12.readout_part, f32[6,256,128]{2,1,0:T(8,128)} %get-tuple-element.13.woven), custom_call_target="tpu_custom_call" | custom-call | tf_op jit(solution)/shard_map/outputs/pallas_call | solution.py:720
